TPU v7x, 32 devices: a whole 2x2x4 slice. The times are simulated.
32 devices in a mesh: dp: 4 (over y, x), seq: 4 (over z), head: 2 (over core).
Axes of the slice: x: 2, y: 2, z: 4, core: 2. Of those that a mesh axis runs over, the one named last changes fastest.
Arguments:
- latents: bfloat16 [4, 1024, 2048], P('dp', 'seq'), may hold values from -6 to 6
- w_qkv: bfloat16 [2048, 3, 1536], P(None, None, 'head'), may hold values from -0.125 to 0.125
- q_gain: float32 [128], replicated, may hold values from 0.1 to 1.9
- k_gain: float32 [128], replicated, may hold values from 0.1 to 1.9
- neighbours: int32 [16, 9], replicated, may hold values from -1 to 15, as said below
- grad_out: bfloat16 [4, 1024, 1536], P('dp', 'seq', 'head'), may hold values from -6 to 6
Outputs:
- attn_out: bfloat16 [4, 1024, 1536], P('dp', 'seq', 'head')
- grad_x: bfloat16 [4, 1024, 2048], P('dp', ('seq', 'head'))
- grad_w: float32 [2048, 3, 1536], P(('dp', 'seq'), None, 'head')
Inputs may be any that keep to these rules, and one draw needn't show every extreme that they name: `neighbours`: row t lists only tiles whose slab differs from that of t (t // 4) by at most one and whose position in the slab (index % 4) differs by at most one, each at most once; t itself is always listed.
All inputs are finite; a program needn't handle non-finite values.
Results may differ from a plain program's by a relative error of at most 0.017.
Values may be sent and summed in bfloat16 or wider, within the bound.
A program may use at most 128 MiB of HBM per device.

v0:
```python
import functools
import math

import jax
import jax.numpy as jnp
from jax import lax
from jax.experimental import pallas as pl
from jax.experimental.pallas import tpu as pltpu
from jax.sharding import PartitionSpec as P

MESH = pl.DeviceIdType.MESH

HD = 128
TILE = 64


EPS = 1e-06


def inv_rms(values):
    return lax.rsqrt(jnp.mean(values * values, axis=-1, keepdims=True) + EPS)


def norm_back(raw, inverse, gain, upstream):
    normed = raw * inverse
    weighted = upstream * gain
    return inverse * (weighted - normed * jnp.mean(weighted * normed, axis=-1, keepdims=True))


def remote(src, dst, send_sem, recv_sem, peer):
    return pltpu.make_async_remote_copy(
        src_ref=src,
        dst_ref=dst,
        send_sem=send_sem,
        recv_sem=recv_sem,
        device_id=peer,
        device_id_type=MESH,
    )


def layer_kernel(
    n_dp, n_seq, n_head, lat_ref, w_ref, qg_ref, kg_ref, near_ref, do_ref,
    out_ref, gw_ref, gx_ref,
    d_ref, latt_ref, gath, part, flow, gx_acc, gx_recv, lat_buf, w_buf, do_buf, q_raw, k_raw, q_hat, k_hat, v_hat, mask, mask_t, stat, stat_t, clip_buf,
    l_sem, w_sem, a_ss, a_rs, f_ss, f_rs, o_ss, o_rs, s_ss, s_rs, c_ss, c_rs,
    d_ss, d_rs, z_ss, z_rs, h_ss, h_rs,
):
    three, model_width, head_width = w_ref.shape
    slab = lat_ref.shape[0]
    chunks, _, width = d_ref.shape
    parts = chunks // three
    group = width // HD
    heads = head_width // HD
    half = slab // n_head
    block = model_width // n_dp
    scale = 1.0 / math.sqrt(HD)
    me_dp = lax.axis_index("dp")
    me_seq = lax.axis_index("seq")
    me_head = lax.axis_index("head")
    below = me_seq > 0
    above = me_seq < n_seq - 1

    def dp_peer(step, sign=1):
        if n_dp == 4:
            low, high = lax.rem(me_dp, 2), me_dp // 2
            if step % 2:
                low = 1 - low
            if step // 2:
                high = 1 - high
            return high * 2 + low
        return lax.rem(me_dp + n_dp + sign * step, n_dp)

    def head_peer(step, sign=1):
        return lax.rem(me_head + n_head + sign * step, n_head)

    own_lat = pltpu.make_async_copy(lat_ref, lat_buf.at[1], l_sem.at[0])
    own_do = pltpu.make_async_copy(do_ref, do_buf.at[1], l_sem.at[1])

    def cols(p):
        return pl.ds(pl.multiple_of(p * width, width), width)

    def w_copy(c):
        at = cols(lax.rem(c, parts))
        return pltpu.make_async_copy(
            w_ref.at[c // parts, :, at], w_buf.at[c // parts, :, at], w_sem.at[c]
        )

    own_lat.start()

    @pl.loop(0, chunks)
    def _(c):
        w_copy(c).start()

    own_do.start()

    barrier = pltpu.get_barrier_semaphore()

    @pl.when(below)
    def _():
        pl.semaphore_signal(barrier, inc=1, device_id={"seq": me_seq - 1}, device_id_type=MESH)

    @pl.when(above)
    def _():
        pl.semaphore_signal(barrier, inc=1, device_id={"seq": me_seq + 1}, device_id_type=MESH)

    for step in range(1, n_dp):
        pl.semaphore_signal(
            barrier, inc=1, device_id={"dp": dp_peer(step, -1)}, device_id_type=MESH
        )
    for step in range(1, n_head):
        pl.semaphore_signal(
            barrier, inc=1, device_id={"head": head_peer(step, -1)}, device_id_type=MESH
        )
    sides = jnp.minimum(me_seq, 1) + jnp.minimum(n_seq - 1 - me_seq, 1)
    pl.semaphore_wait(barrier, n_dp - 1 + n_head - 1 + sides)

    my_rows = pl.ds(pl.multiple_of(me_head * half, half), half)

    def lat_copy(side):
        return remote(
            lat_ref.at[my_rows], lat_buf.at[2 - 2 * side, my_rows],
            a_ss.at[side], a_rs.at[side], {"seq": me_seq + 2 * side - 1},
        )

    def do_copy(side):
        return remote(
            do_ref, do_buf.at[2 - 2 * side],
            o_ss.at[side], o_rs.at[side], {"seq": me_seq + 2 * side - 1},
        )

    def stat_copy(side):
        return remote(
            stat_t.at[1], stat_t.at[2 - 2 * side],
            s_ss.at[side], s_rs.at[side], {"seq": me_seq + 2 * side - 1},
        )

    def pass_copy(slot, step):
        return remote(
            lat_buf.at[slot, my_rows], lat_buf.at[slot, my_rows],
            f_ss.at[slot // 2, step - 1], f_rs.at[slot // 2, step - 1],
            {"head": head_peer(step)},
        )

    def clip_copy(step):
        peer = dp_peer(step)
        return remote(
            lat_ref.at[:, pl.ds(pl.multiple_of(peer * block, block), block)],
            clip_buf.at[step - 1], c_ss.at[step - 1], c_rs.at[step - 1], {"dp": peer},
        )

    @pl.when(below)
    def _():
        lat_copy(0).start()

    @pl.when(above)
    def _():
        lat_copy(1).start()

    for step in range(1, n_dp):
        clip_copy(step).start()

    @pl.when(below)
    def _():
        do_copy(0).start()

    @pl.when(above)
    def _():
        do_copy(1).start()

    def clear(slot):
        lat_buf[slot] = jnp.zeros_like(lat_buf[slot])
        do_buf[slot] = jnp.zeros_like(do_buf[slot])
        stat_t[slot] = jnp.ones_like(stat_t[slot])

    @pl.when(me_seq == 0)
    def _():
        clear(0)

    @pl.when(me_seq == n_seq - 1)
    def _():
        clear(2)

    tiles = near_ref.shape[0]
    near = near_ref[...]
    tile_ids = lax.broadcasted_iota(jnp.int32, (tiles, tiles), 1)
    hits = jnp.zeros((tiles, tiles), jnp.float32)
    for slot in range(near_ref.shape[1]):
        hits = jnp.where(near[:, slot : slot + 1] == tile_ids, 1.0, hits)
    hits = hits.astype(jnp.bfloat16)
    own_tile = me_seq * (slab // TILE)
    first_tile = own_tile - slab // TILE
    own_pick = lax.broadcasted_iota(jnp.int32, (slab, tiles), 1) == (
        lax.broadcasted_iota(jnp.int32, (slab, tiles), 0) // TILE + own_tile
    )
    own_pick = jnp.where(own_pick, 1.0, 0.0).astype(jnp.bfloat16)
    wide_pick = lax.broadcasted_iota(jnp.int32, (tiles, 3 * slab), 0) == (
        lax.broadcasted_iota(jnp.int32, (tiles, 3 * slab), 1) // TILE + first_tile
    )
    wide_pick = jnp.where(wide_pick, 1.0, 0.0).astype(jnp.bfloat16)
    picked = jnp.dot(own_pick, hits, preferred_element_type=jnp.float32).astype(jnp.bfloat16)
    mask[...] = jnp.dot(picked, wide_pick, preferred_element_type=jnp.float32)
    picked = lax.dot_general(
        own_pick, hits, (((1,), (1,)), ((), ())), preferred_element_type=jnp.float32
    ).astype(jnp.bfloat16)
    mask_t[...] = jnp.dot(picked, wide_pick, preferred_element_type=jnp.float32)

    q_gain = qg_ref[...]
    k_gain = kg_ref[...]
    own_lat.wait()

    def arrive(slot, side):
        lat_copy(side).wait_recv()
        for step in range(1, n_head):
            pass_copy(slot, step).start()

    def passed(slot):
        for step in range(1, n_head):
            pass_copy(slot, step).wait_recv()

    @pl.loop(0, 3)
    def _(turn):
        slot = lax.rem(turn + 1, 3)

        @pl.when(turn == 1)
        def _():
            @pl.when(above)
            def _():
                arrive(2, 0)

            @pl.when(below)
            def _():
                arrive(0, 1)

            @pl.when(above)
            def _():
                passed(2)

        @pl.when((turn == 2) & below)
        def _():
            passed(0)

        for kind in range(three):
            @pl.loop(0, parts)
            def _(p):
                @pl.when(turn == 0)
                def _():
                    w_copy(kind * parts + p).wait()

                raw = jnp.dot(
                    lat_buf[slot], w_buf[kind, :, cols(p)], preferred_element_type=jnp.float32
                )
                if kind == 2:
                    v_hat[slot, :, cols(p)] = raw.astype(jnp.bfloat16)
                else:
                    kept, normed, gain = ((q_raw, q_hat, q_gain), (k_raw, k_hat, k_gain))[kind]

                    @pl.when(turn == 0)
                    def _():
                        kept[:, cols(p)] = raw

                    pieces = []
                    for h in range(group):
                        piece = raw[:, h * HD : (h + 1) * HD]
                        pieces.append((piece * inv_rms(piece) * gain).astype(jnp.bfloat16))
                    normed[slot, :, cols(p)] = jnp.concatenate(pieces, axis=1)

    def at(h):
        return pl.ds(pl.multiple_of(h * HD, HD), HD)

    def nt(a, b):
        return lax.dot_general(a, b, (((1,), (1,)), ((), ())), preferred_element_type=jnp.float32)

    def put(position, h, value):
        d_ref[position, :, at(lax.rem(h, group))] = value.astype(jnp.bfloat16)

    def place(position):
        late = jnp.maximum(position - parts, 0)
        is_late = jnp.where(position >= parts, 1, 0)
        kind = is_late * (1 + lax.rem(late, 2))
        p = is_late * (late // 2) + (1 - is_late) * position
        return kind, cols(p)

    relay = n_dp == 4
    direct = (1, 2) if relay else tuple(range(1, n_dp))
    rows = gw_ref.shape[1]

    def dp_copy(c, step):
        return remote(
            d_ref.at[c], gath.at[c, step - 1],
            d_ss.at[c, step - 1], d_rs.at[c, step - 1], {"dp": dp_peer(step)},
        )

    def relay_copy(c, via, onward):
        return remote(
            gath.at[c, via - 1], gath.at[c, 2],
            d_ss.at[c, 2], d_rs.at[c, 2], {"dp": dp_peer(onward)},
        )

    def hop(side, c, t):
        peer = lax.rem(me_seq + n_seq + 1 - 2 * side, n_seq)
        return remote(
            flow.at[side, c, t], flow.at[side, c, t],
            z_ss.at[side, c, t], z_rs.at[side, c, t], {"seq": peer},
        )

    fed = (below, above)

    def onward(side, t):
        return t < me_seq if side else t > me_seq

    def stage(side, c):
        @pl.loop(0, n_seq)
        def _(turn):
            t = turn if side else n_seq - 1 - turn

            @pl.when(onward(side, t))
            def _():
                @pl.when(fed[side])
                def _():
                    hop(side, c, t).wait_recv()
                    summed = part[c, t] + flow[side, c, t].astype(jnp.float32)
                    flow[side, c, t] = summed.astype(jnp.bfloat16)

                @pl.when(jnp.logical_not(fed[side]))
                def _():
                    flow[side, c, t] = part[c, t].astype(jnp.bfloat16)

                hop(side, c, t).start()

    def send_own(c):
        for step in direct:
            dp_copy(c, step).start()

    def pass_on(c):
        for step in direct:
            dp_copy(c, step).wait_recv()
        if relay:
            @pl.when(lax.rem(c, 2) == 0)
            def _():
                relay_copy(c, 1, 2).start()

            @pl.when(lax.rem(c, 2) == 1)
            def _():
                relay_copy(c, 2, 1).start()

    def input_share(c):
        kind, where = place(c)
        gx_acc[...] += nt(d_ref[c], w_buf[kind, :, where])

    def weight_share(c):
        if relay:
            relay_copy(c, 1, 2).wait_recv()
        others = gath[c].reshape((n_dp - 1) * slab, width)
        product = jnp.dot(latt_ref[:, :slab], d_ref[c], preferred_element_type=jnp.float32)
        product += jnp.dot(latt_ref[:, slab:], others, preferred_element_type=jnp.float32)
        part[c] = product.reshape(n_seq, rows, width)

    own_do.wait()
    lanes = lax.broadcasted_iota(jnp.int32, (slab, 128), 1)
    stat[...] = jnp.zeros_like(stat)

    @pl.loop(0, heads)
    def _(h):
        queries = q_hat[1, :, at(h)]
        keys = k_hat[:, :, at(h)].reshape(3 * slab, HD)
        values = v_hat[:, :, at(h)].reshape(3 * slab, HD)
        expo = jnp.exp(nt(queries, keys) * scale) * mask[...]
        row_total = jnp.sum(expo, axis=-1, keepdims=True)
        probs = expo * (1.0 / row_total)
        out_ref[:, at(h)] = jnp.dot(
            probs.astype(jnp.bfloat16), values, preferred_element_type=jnp.float32
        ).astype(jnp.bfloat16)
        d_probs = nt(do_buf[1, :, at(h)], values)
        row_delta = jnp.sum(probs * d_probs, axis=-1, keepdims=True)
        d_scores = (probs * (d_probs - row_delta) * scale).astype(jnp.bfloat16)
        d_qhat = jnp.dot(d_scores, keys, preferred_element_type=jnp.float32)
        raw = q_raw[:, at(h)]
        put(h // group, h, norm_back(raw, inv_rms(raw), q_gain, d_qhat))
        rows = jnp.where(lanes == 2 * h, row_total, stat[...])
        stat[...] = jnp.where(lanes == 2 * h + 1, row_delta, rows)

        @pl.when(lax.rem(h, group) == group - 1)
        def _():
            send_own(h // group)

    stat_t[1] = jnp.transpose(stat[...])[: stat_t.shape[1]]

    @pl.when(below)
    def _():
        stat_copy(0).start()

    @pl.when(above)
    def _():
        stat_copy(1).start()

    own_cols = pl.ds(pl.multiple_of(me_dp * block, block), block)
    latt_ref[:, :slab] = jnp.transpose(lat_buf[1, :, own_cols])
    for step in range(1, n_dp):
        clip_copy(step).wait_recv()
        latt_ref[:, step * slab : (step + 1) * slab] = jnp.transpose(clip_buf[step - 1])

    gx_acc[...] = jnp.zeros_like(gx_acc)

    def reverse(h):
        keys = k_hat[1, :, at(h)]
        values = v_hat[1, :, at(h)]
        queries = q_hat[:, :, at(h)].reshape(3 * slab, HD)
        upstream = do_buf[:, :, at(h)].reshape(3 * slab, HD)
        total = jnp.concatenate([stat_t[s, pl.ds(2 * h, 1), :] for s in range(3)], axis=1)
        delta = jnp.concatenate([stat_t[s, pl.ds(2 * h + 1, 1), :] for s in range(3)], axis=1)
        probs = jnp.exp(nt(keys, queries) * scale) * mask_t[...] * (1.0 / total)
        late = parts + 2 * (h // group)
        put(late + 1, h, jnp.dot(probs.astype(jnp.bfloat16), upstream, preferred_element_type=jnp.float32))
        d_scores = (probs * (nt(values, upstream) - delta) * scale).astype(jnp.bfloat16)
        d_khat = jnp.dot(d_scores, queries, preferred_element_type=jnp.float32)
        raw = k_raw[:, at(h)]
        put(late, h, norm_back(raw, inv_rms(raw), k_gain, d_khat))

    share = gx_ref.shape[0]

    def h_copy(step):
        peer = head_peer(step)
        return remote(
            gx_acc.at[pl.ds(pl.multiple_of(peer * share, share), share)],
            gx_recv.at[step - 1], h_ss.at[step - 1], h_rs.at[step - 1], {"head": peer},
        )

    @pl.loop(0, chunks + n_seq - 1)
    def _(tick):
        @pl.when(tick < chunks)
        def _():
            pass_on(tick)

        @pl.when((tick > 0) & (tick < chunks - parts))
        def _():
            send_own(tick + parts)

        @pl.when((tick > 0) & (tick <= chunks))
        def _():
            weight_share(tick - 1)

        for side in range(2):
            lag = n_seq - 1 - me_seq if side else me_seq
            c = tick - 1 - lag

            @pl.when((c >= 0) & (c < chunks))
            def _():
                stage(side, c)

        @pl.when((tick == 0) & above)
        def _():
            do_copy(0).wait_recv()
            stat_copy(0).wait_recv()

        @pl.when((tick == 0) & below)
        def _():
            do_copy(1).wait_recv()
            stat_copy(1).wait_recv()

        @pl.when(tick < parts)
        def _():
            @pl.loop(0, group)
            def _(h):
                reverse(tick * group + h)

        @pl.when(tick == 0)
        def _():
            send_own(parts)

        @pl.when(tick < chunks)
        def _():
            input_share(tick)

        @pl.when(tick == chunks - 1)
        def _():
            for step in range(1, n_head):
                h_copy(step).start()


    for step in range(1, n_head):
        h_copy(step).wait()
    total = gx_acc[pl.ds(pl.multiple_of(me_head * share, share), share)]
    for step in range(1, n_head):
        total = total + gx_recv[step - 1]
    gx_ref[...] = total.astype(gx_ref.dtype)

    @pl.loop(0, chunks)
    def _(c):
        kind, where = place(c)
        gw_ref[kind, :, where] = part[c, me_seq]
        for side in range(2):
            @pl.when(fed[side])
            def _():
                hop(side, c, me_seq).wait_recv()
                gw_ref[kind, :, where] += flow[side, c, me_seq].astype(jnp.float32)

            @pl.loop(0, n_seq)
            def _(t):
                @pl.when(onward(side, t))
                def _():
                    hop(side, c, t).wait_send()

        for step in direct:
            dp_copy(c, step).wait_send()
        if relay:
            relay_copy(c, 1, 2).wait_send()

    def settle(slot, side):
        lat_copy(side).wait_send()
        do_copy(side).wait_send()
        stat_copy(side).wait_send()
        for step in range(1, n_head):
            pass_copy(slot, step).wait_send()

    @pl.when(below)
    def _():
        settle(0, 0)

    @pl.when(above)
    def _():
        settle(2, 1)

    for step in range(1, n_dp):
        clip_copy(step).wait_send()


def layer(slab_tokens, w_three, q_gain, k_gain, neighbours, upstream):
    n_dp, n_seq, n_head = (lax.axis_size(axis) for axis in ("dp", "seq", "head"))
    slab = slab_tokens.shape[0]
    three, model_width, head_width = w_three.shape
    heads = head_width // HD
    group = 3 if heads % 3 == 0 else 1
    width = group * HD
    chunks = three * heads // group
    block = model_width // n_dp
    rows = block // n_seq
    share = slab // n_head
    stat_rows = -(-2 * heads // 8) * 8
    vmem = pl.BlockSpec(memory_space=pltpu.VMEM)
    anywhere = pl.BlockSpec(memory_space=pl.ANY)
    dma = pltpu.SemaphoreType.DMA
    bf16, f32 = jnp.bfloat16, jnp.float32
    return pl.pallas_call(
        functools.partial(layer_kernel, n_dp, n_seq, n_head),
        out_shape=(
            jax.ShapeDtypeStruct((slab, head_width), bf16),
            jax.ShapeDtypeStruct((three, rows, head_width), f32),
            jax.ShapeDtypeStruct((share, model_width), bf16),
        ),
        in_specs=[anywhere, anywhere, vmem, vmem, vmem, anywhere],
        out_specs=(vmem, vmem, vmem),
        scratch_shapes=[
            pltpu.VMEM((chunks, slab, width), bf16),
            pltpu.VMEM((block, n_dp * slab), bf16),
            pltpu.VMEM((chunks, n_dp - 1, slab, width), bf16),
            pltpu.VMEM((chunks, n_seq, rows, width), f32),
            pltpu.VMEM((2, chunks, n_seq, rows, width), bf16),
            pltpu.VMEM((slab, model_width), f32),
            pltpu.VMEM((n_head - 1, share, model_width), f32),
            pltpu.VMEM((3, slab, model_width), bf16),
            pltpu.VMEM((three, model_width, head_width), bf16),
            pltpu.VMEM((3, slab, head_width), bf16),
            pltpu.VMEM((slab, head_width), f32),
            pltpu.VMEM((slab, head_width), f32),
            pltpu.VMEM((3, slab, head_width), bf16),
            pltpu.VMEM((3, slab, head_width), bf16),
            pltpu.VMEM((3, slab, head_width), bf16),
            pltpu.VMEM((slab, 3 * slab), f32),
            pltpu.VMEM((slab, 3 * slab), f32),
            pltpu.VMEM((slab, 128), f32),
            pltpu.VMEM((3, stat_rows, slab), f32),
            pltpu.VMEM((n_dp - 1, slab, block), bf16),
            dma((2,)),
            dma((chunks,)),
            dma((2,)),
            dma((2,)),
            dma((2, n_head - 1)),
            dma((2, n_head - 1)),
            dma((2,)),
            dma((2,)),
            dma((2,)),
            dma((2,)),
            dma((n_dp - 1,)),
            dma((n_dp - 1,)),
            dma((chunks, n_dp - 1)),
            dma((chunks, n_dp - 1)),
            dma((2, chunks, n_seq)),
            dma((2, chunks, n_seq)),
            dma((n_head - 1,)),
            dma((n_head - 1,)),
        ],
        compiler_params=pltpu.CompilerParams(
            collective_id=0, has_side_effects=True, vmem_limit_bytes=60 * 1024 * 1024
        ),
        name="layer",
    )(slab_tokens, w_three, q_gain.reshape(1, HD), k_gain.reshape(1, HD), neighbours, upstream)


def local(latents, w_qkv, q_gain, k_gain, neighbours, grad_out):
    w_three = jnp.transpose(w_qkv, (1, 0, 2))
    attn_out, grad_w, grad_x = layer(
        latents[0], w_three, q_gain, k_gain, neighbours, grad_out[0]
    )
    return (attn_out[None], grad_x[None], jnp.transpose(grad_w, (1, 0, 2)))


def solution(mesh):
    in_specs = (P("dp", "seq", None), P(None, None, "head"), P(), P(), P(), P("dp", "seq", "head"))
    out_specs = (
        P("dp", "seq", "head"),
        P("dp", ("seq", "head"), None),
        P(("dp", "seq"), None, "head"),
    )
    return jax.shard_map(local, mesh=mesh, in_specs=in_specs, out_specs=out_specs, check_vma=False)
```

profile of v0, /device:TPU:0, one launch (start us, length us, event | category | flops | bytes accessed | tf_op | source)
XLA Modules:
  0.0 100.2 jit_solution(14431721830561828302)
XLA Ops:
  0.6 94.8 %layer.1 = (bf16[256,768]{1,0:T(8,128)(2,1)}, f32[3,128,768]{2,1,0:T(8,128)}, bf16[128,2048]{1,0:T(8,128)(2,1)}) custom-call(bf16[256,2048]{1,0:T(8,128)(2,1)} %bitcast.10, bf16[3,2048,768]{2,1,0:T(8,128)(2,1)} %bitcast.8, f32[1,128]{1,0:T(1,128)} %bitcast.14, f32[1,128]{1,0:T(1,128)} %bitcast.15, s32[16,9]{1,0:T(8,128)} %near_ref.1, bf16[256,768]{1,0:T(8,128)(2,1)} %bitcast.12), custom_call_target="tpu_custom_call" | custom-call | tf_op jit(solution)/shard_map/layer/pallas_call | solution.py:543
  95.5 0.0 copy-start
  95.5 1.9 %copy.12 = bf16[1,256,768]{2,1,0:T(8,128)(2,1)} copy(bf16[1,256,768]{2,1,0:T(8,128)(2,1)} %bitcast.13) | data formatting | bytes 786432
  97.4 1.9 %copy.13 = bf16[1,128,2048]{2,1,0:T(8,128)(2,1)} copy(bf16[1,128,2048]{2,1,0:T(8,128)(2,1)} %bitcast.11) | data formatting | bytes 1048576
  99.2 0.0 copy-done
  99.2 1.0 %copy.14 = f32[128,3,768]{2,0,1:T(8,128)} copy(f32[128,3,768]{2,0,1:T(8,128)S(1)} %bitcast.9) | data formatting | bytes 2359296
Async XLA Ops:
  95.5 3.8 %copy-start = (f32[3,128,768]{2,1,0:T(8,128)S(1)}, f32[3,128,768]{2,1,0:T(8,128)}, u32[]{:S(2)}) copy-start(f32[3,128,768]{2,1,0:T(8,128)} %get-tuple-element.8) | copy-start | bytes 3538948
where the time goes:
time: 100 us
  Pallas kernels  94.8 us (95%)
  local copies, waits for them, and re-layouts  4.76 us (5%)
    pallas_call x1, Pallas kernels, layer(): pl.pallas_call(functools.partial(layer_kernel, n_dp, n_seq, n_head), out_...  94.8 us
    unnamed x5, local copies, waits for them, and re-layouts  4.76 us

commit v1 on v0

v1 whole, which is shorter than its diff:
```python
import contextlib
import functools
import math

import jax
import jax.numpy as jnp
from jax import lax
from jax.experimental import pallas as pl
from jax.experimental.pallas import tpu as pltpu
from jax.sharding import PartitionSpec as P

MESH = pl.DeviceIdType.MESH

HD = 128
TILE = 64
PIECES = 2
AHEAD = 2


EPS = 1e-06


def scope(name):
    return contextlib.nullcontext()


def inv_rms(values):
    return lax.rsqrt(jnp.mean(values * values, axis=-1, keepdims=True) + EPS)


def norm_back(raw, inverse, gain, upstream):
    normed = raw * inverse
    weighted = upstream * gain
    return inverse * (weighted - normed * jnp.mean(weighted * normed, axis=-1, keepdims=True))


def nt(a, b):
    return lax.dot_general(a, b, (((1,), (1,)), ((), ())), preferred_element_type=jnp.float32)


def remote(src, dst, send_sem, recv_sem, peer):
    return pltpu.make_async_remote_copy(
        src_ref=src,
        dst_ref=dst,
        send_sem=send_sem,
        recv_sem=recv_sem,
        device_id=peer,
        device_id_type=MESH,
    )


def layer_kernel(
    n_dp, n_seq, n_head, lat_ref, w_ref, qg_ref, kg_ref, near_ref, do_ref,
    out_ref, gw_ref, gx_ref,
    gath, latt_ref, part, flow, gx_acc, gx_recv, gx_buf, lat_own, halo, w_buf, do_buf,
    q_raw, k_raw, q_hat, k_hat, v_hat, mask, mask_t, stat, stat_t, clip_buf, out_buf, gw_buf,
    qg_buf, kg_buf, near_buf,
    l_sem, w_sem, a_ss, a_rs, f_ss, f_rs, o_ss, o_rs, s_ss, s_rs, c_ss, c_rs,
    d_ss, d_rs, z_ss, z_rs, h_ss, h_rs, out_sem, gw_sem, gx_sem,
):
    three, model_width, head_width = w_ref.shape
    slab = lat_ref.shape[0]
    items = gath.shape[0]
    chunks, _, rows, width = part.shape
    group = width // HD
    parts = chunks // three
    heads = head_width // HD
    pieces, _, piece, _ = halo.shape
    sub = piece // n_head
    block = model_width // n_dp
    scale = 1.0 / math.sqrt(HD)
    me_dp = lax.axis_index("dp")
    me_seq = lax.axis_index("seq")
    me_head = lax.axis_index("head")
    below = me_seq > 0
    above = me_seq < n_seq - 1

    def dp_peer(step, sign=1):
        if n_dp == 4:
            low, high = lax.rem(me_dp, 2), me_dp // 2
            if step % 2:
                low = 1 - low
            if step // 2:
                high = 1 - high
            return high * 2 + low
        return lax.rem(me_dp + n_dp + sign * step, n_dp)

    def head_peer(step, sign=1):
        return lax.rem(me_head + n_head + sign * step, n_head)

    def cols(p):
        return pl.ds(pl.multiple_of(p * width, width), width)

    def at(h):
        return pl.ds(pl.multiple_of(h * HD, HD), HD)

    barrier = pltpu.get_barrier_semaphore()

    @pl.when(below)
    def _():
        pl.semaphore_signal(barrier, inc=1, device_id={"seq": me_seq - 1}, device_id_type=MESH)

    @pl.when(above)
    def _():
        pl.semaphore_signal(barrier, inc=1, device_id={"seq": me_seq + 1}, device_id_type=MESH)

    for step in range(1, n_dp):
        pl.semaphore_signal(
            barrier, inc=1, device_id={"dp": dp_peer(step, -1)}, device_id_type=MESH
        )
    for step in range(1, n_head):
        pl.semaphore_signal(
            barrier, inc=1, device_id={"head": head_peer(step, -1)}, device_id_type=MESH
        )

    own_lat = pltpu.make_async_copy(lat_ref, lat_own, l_sem.at[0])
    own_do = pltpu.make_async_copy(do_ref, do_buf.at[1], l_sem.at[1])
    small = [
        pltpu.make_async_copy(near_ref, near_buf, l_sem.at[2]),
        pltpu.make_async_copy(qg_ref, qg_buf, l_sem.at[3]),
        pltpu.make_async_copy(kg_ref, kg_buf, l_sem.at[4]),
    ]

    def w_copy(kind, p):
        return pltpu.make_async_copy(
            w_ref.at[kind, :, cols(p)], w_buf.at[kind, :, cols(p)], w_sem.at[kind * parts + p]
        )

    for copy in small:
        copy.start()
    own_lat.start()
    for kind in range(three):
        @pl.loop(0, parts)
        def _(p):
            w_copy(kind, p).start()
    own_do.start()

    for copy in small:
        copy.wait()
    tiles = near_ref.shape[0]
    near = near_buf[...]
    tile_ids = lax.broadcasted_iota(jnp.int32, (tiles, tiles), 1)
    hits = jnp.zeros((tiles, tiles), jnp.float32)
    for slot in range(near_ref.shape[1]):
        hits = jnp.where(near[:, slot : slot + 1] == tile_ids, 1.0, hits)
    hits = hits.astype(jnp.bfloat16)
    own_tile = me_seq * (slab // TILE)
    first_tile = own_tile - slab // TILE
    own_pick = lax.broadcasted_iota(jnp.int32, (slab, tiles), 1) == (
        lax.broadcasted_iota(jnp.int32, (slab, tiles), 0) // TILE + own_tile
    )
    own_pick = jnp.where(own_pick, 1.0, 0.0).astype(jnp.bfloat16)
    wide_pick = lax.broadcasted_iota(jnp.int32, (tiles, 3 * slab), 0) == (
        lax.broadcasted_iota(jnp.int32, (tiles, 3 * slab), 1) // TILE + first_tile
    )
    wide_pick = jnp.where(wide_pick, 1.0, 0.0).astype(jnp.bfloat16)
    picked = jnp.dot(own_pick, hits, preferred_element_type=jnp.float32).astype(jnp.bfloat16)
    mask[...] = jnp.dot(picked, wide_pick, preferred_element_type=jnp.float32)
    picked = lax.dot_general(
        own_pick, hits, (((1,), (1,)), ((), ())), preferred_element_type=jnp.float32
    ).astype(jnp.bfloat16)
    mask_t[...] = jnp.dot(picked, wide_pick, preferred_element_type=jnp.float32)

    def clear(side):
        for j in range(pieces):
            halo[j, side] = jnp.zeros_like(halo[j, side])
        do_buf[2 * side] = jnp.zeros_like(do_buf[2 * side])
        stat_t[2 * side] = jnp.ones_like(stat_t[2 * side])

    @pl.when(me_seq == 0)
    def _():
        clear(0)

    @pl.when(me_seq == n_seq - 1)
    def _():
        clear(1)

    q_gain = qg_buf[...]
    k_gain = kg_buf[...]

    sides = jnp.minimum(me_seq, 1) + jnp.minimum(n_seq - 1 - me_seq, 1)
    with scope("BARRIER"):
        pl.semaphore_wait(barrier, n_dp - 1 + n_head - 1 + sides)

    sub_rows = pl.ds(pl.multiple_of(me_head * sub, sub), sub)

    def lat_copy(side, j):
        return remote(
            lat_ref.at[pl.ds(pl.multiple_of(j * piece + me_head * sub, sub), sub)],
            halo.at[j, 1 - side, sub_rows],
            a_ss.at[side, j], a_rs.at[side, j], {"seq": me_seq + 2 * side - 1},
        )

    def do_copy(side):
        return remote(
            do_ref, do_buf.at[2 - 2 * side],
            o_ss.at[side], o_rs.at[side], {"seq": me_seq + 2 * side - 1},
        )

    def stat_copy(side):
        return remote(
            stat_t.at[1], stat_t.at[2 - 2 * side],
            s_ss.at[side], s_rs.at[side], {"seq": me_seq + 2 * side - 1},
        )

    def pass_copy(side, j, step):
        return remote(
            halo.at[j, side, sub_rows], halo.at[j, side, sub_rows],
            f_ss.at[side, j, step - 1], f_rs.at[side, j, step - 1],
            {"head": head_peer(step)},
        )

    def clip_copy(step):
        peer = dp_peer(step)
        return remote(
            lat_ref.at[:, pl.ds(pl.multiple_of(peer * block, block), block)],
            clip_buf.at[step - 1], c_ss.at[step - 1], c_rs.at[step - 1], {"dp": peer},
        )

    for j in range(pieces):
        @pl.when(below)
        def _():
            lat_copy(0, j).start()

        @pl.when(above)
        def _():
            lat_copy(1, j).start()

    for step in range(1, n_dp):
        clip_copy(step).start()

    @pl.when(below)
    def _():
        do_copy(0).start()

    @pl.when(above)
    def _():
        do_copy(1).start()

    def normed(raw, gain):
        found = []
        for h in range(group):
            head = raw[:, h * HD : (h + 1) * HD]
            found.append((head * inv_rms(head) * gain).astype(jnp.bfloat16))
        return jnp.concatenate(found, axis=1)

    own_lat.wait()

    for kind in range(three):
        with scope("OWN%d" % kind):
            @pl.loop(0, parts)
            def _(p):
                w_copy(kind, p).wait()
                raw = jnp.dot(
                    lat_own[...], w_buf[kind, :, cols(p)], preferred_element_type=jnp.float32
                )
                if kind == 0:
                    q_raw[:, cols(p)] = raw
                    q_hat[1, :, cols(p)] = normed(raw, q_gain)
                elif kind == 1:
                    k_raw[:, cols(p)] = raw
                    k_hat[1, :, cols(p)] = normed(raw, k_gain)
                else:
                    v_hat[1, :, cols(p)] = raw.astype(jnp.bfloat16)

    def arrive(j):
        @pl.when(above)
        def _():
            lat_copy(0, j).wait_recv()
            for step in range(1, n_head):
                pass_copy(1, j, step).start()

        @pl.when(below)
        def _():
            lat_copy(1, j).wait_recv()
            for step in range(1, n_head):
                pass_copy(0, j, step).start()

        @pl.when(above)
        def _():
            for step in range(1, n_head):
                pass_copy(1, j, step).wait_recv()

        @pl.when(below)
        def _():
            for step in range(1, n_head):
                pass_copy(0, j, step).wait_recv()

    def halo_part(kind, j, p):
        raw = jnp.dot(
            halo[j].reshape(2 * piece, model_width), w_buf[kind, :, cols(p)],
            preferred_element_type=jnp.float32,
        )
        if kind == 2:
            kept, value = v_hat, raw.astype(jnp.bfloat16)
        else:
            kept, value = ((q_hat, k_hat)[kind], normed(raw, (q_gain, k_gain)[kind]))
        at_rows = slice(j * piece, (j + 1) * piece)
        kept[0, at_rows, cols(p)] = value[:piece]
        kept[2, at_rows, cols(p)] = value[piece:]

    for j in range(pieces - 1):
        with scope("ARRIVE%d" % j):
            arrive(j)
        for kind in (1, 2, 0):
            with scope("HALO%d" % kind):
                @pl.loop(0, parts)
                def _(p):
                    halo_part(kind, j, p)

    with scope("ARRIVEL"):
        arrive(pieces - 1)

    def put(item, value):
        gath[item, 0] = value.astype(jnp.bfloat16)

    def place(position):
        late = jnp.maximum(position - parts, 0)
        is_late = jnp.where(position >= parts, 1, 0)
        kind = is_late * (1 + lax.rem(late, 2))
        p = is_late * (late // 2) + (1 - is_late) * position
        return kind, cols(p)

    relay = n_dp == 4
    direct = (1, 2) if relay else tuple(range(1, n_dp))
    half = slab // 2
    first, second = slice(0, half), slice(half, slab)

    def dp_copy(i, step):
        return remote(
            gath.at[i, 0], gath.at[i, step],
            d_ss.at[i, step - 1], d_rs.at[i, step - 1], {"dp": dp_peer(step)},
        )

    def relay_copy(i, via):
        which = (first, second)[via - 1]
        return remote(
            gath.at[i, via, which], gath.at[i, 3, which],
            d_ss.at[i, 1 + via], d_rs.at[i, 1 + via], {"dp": dp_peer(3 - via)},
        )

    def send_own(i):
        for step in direct:
            dp_copy(i, step).start()

    def pass_on(i):
        for step in direct:
            dp_copy(i, step).wait_recv()
            if relay:
                relay_copy(i, step).start()

    def hop(side, c, t):
        peer = lax.rem(me_seq + n_seq + 1 - 2 * side, n_seq)
        return remote(
            flow.at[side, c, t], flow.at[side, c, t],
            z_ss.at[side, c, t], z_rs.at[side, c, t], {"seq": peer},
        )

    fed = (below, above)

    def onward(side, t):
        return t < me_seq if side else t > me_seq

    def stage(side, c):
        @pl.loop(0, n_seq)
        def _(turn):
            t = turn if side else n_seq - 1 - turn

            @pl.when(onward(side, t))
            def _():
                @pl.when(fed[side])
                def _():
                    hop(side, c, t).wait_recv()
                    summed = part[c, t] + flow[side, c, t].astype(jnp.float32)
                    flow[side, c, t] = summed.astype(jnp.bfloat16)

                @pl.when(jnp.logical_not(fed[side]))
                def _():
                    flow[side, c, t] = part[c, t].astype(jnp.bfloat16)

                hop(side, c, t).start()

    def paired(ref, c):
        found = [ref(c * group + j) for j in range(group)]
        return jnp.concatenate(found, axis=1)

    def input_share(c):
        kind, where = place(c)
        gx_acc[...] += nt(paired(lambda i: gath[i, 0], c), w_buf[kind, :, where])

    def weight_share(c):
        if relay:
            for j in range(group):
                for via in (1, 2):
                    relay_copy(c * group + j, via).wait_recv()
        everyone = paired(lambda i: gath[i].reshape(n_dp * slab, HD), c)
        product = jnp.dot(latt_ref[...], everyone, preferred_element_type=jnp.float32)
        part[c] = product.reshape(n_seq, rows, width)

    own_do.wait()
    lanes = lax.broadcasted_iota(jnp.int32, (slab, 128), 1)
    stat[...] = jnp.zeros_like(stat)

    def out_copy(p):
        return pltpu.make_async_copy(
            out_buf.at[:, cols(p)], out_ref.at[:, cols(p)], out_sem.at[p]
        )

    def forward(h):
        queries = q_hat[1, :, at(h)]
        keys = k_hat[:, :, at(h)].reshape(3 * slab, HD)
        values = v_hat[:, :, at(h)].reshape(3 * slab, HD)
        expo = jnp.exp(nt(queries, keys) * scale) * mask[...]
        row_total = jnp.sum(expo, axis=-1, keepdims=True)
        probs = expo * (1.0 / row_total)
        out_buf[:, at(h)] = jnp.dot(
            probs.astype(jnp.bfloat16), values, preferred_element_type=jnp.float32
        ).astype(jnp.bfloat16)
        d_probs = nt(do_buf[1, :, at(h)], values)
        row_delta = jnp.sum(probs * d_probs, axis=-1, keepdims=True)
        d_scores = (probs * (d_probs - row_delta) * scale).astype(jnp.bfloat16)
        d_qhat = jnp.dot(d_scores, keys, preferred_element_type=jnp.float32)
        raw = q_raw[:, at(h)]
        put(h, norm_back(raw, inv_rms(raw), q_gain, d_qhat))
        kept = jnp.where(lanes == 2 * h, row_total, stat[...])
        stat[...] = jnp.where(lanes == 2 * h + 1, row_delta, kept)

    early = max(heads - AHEAD * group, 0)

    @pl.loop(0, parts)
    def _(p):
        with scope("HALOKV"):
            halo_part(1, pieces - 1, p)
            halo_part(2, pieces - 1, p)

        @pl.loop(0, group)
        def _(j):
            h = p * group + j
            with scope("FWD"):
                forward(h)
                send_own(h)

            @pl.when(h >= heads - early)
            def _():
                with scope("PASSE"):
                    pass_on(h - (heads - early))

        out_copy(p).start()

    stat_t[1] = jnp.transpose(stat[...])[: stat_t.shape[1]]

    @pl.when(below)
    def _():
        stat_copy(0).start()

    @pl.when(above)
    def _():
        stat_copy(1).start()

    own_cols = pl.ds(pl.multiple_of(me_dp * block, block), block)
    with scope("CLIP"):
        latt_ref[:, :slab] = jnp.transpose(lat_own[:, own_cols])
        for step in range(1, n_dp):
            clip_copy(step).wait_recv()
            latt_ref[:, step * slab : (step + 1) * slab] = jnp.transpose(clip_buf[step - 1])

    gx_acc[...] = jnp.zeros_like(gx_acc)

    def reverse(h):
        keys = k_hat[1, :, at(h)]
        values = v_hat[1, :, at(h)]
        queries = q_hat[:, :, at(h)].reshape(3 * slab, HD)
        upstream = do_buf[:, :, at(h)].reshape(3 * slab, HD)
        total = jnp.concatenate([stat_t[s, pl.ds(2 * h, 1), :] for s in range(3)], axis=1)
        delta = jnp.concatenate([stat_t[s, pl.ds(2 * h + 1, 1), :] for s in range(3)], axis=1)
        probs = jnp.exp(nt(keys, queries) * scale) * mask_t[...] * (1.0 / total)
        late = (parts + 2 * (h // group)) * group + lax.rem(h, group)
        put(late + group, jnp.dot(probs.astype(jnp.bfloat16), upstream, preferred_element_type=jnp.float32))
        d_scores = (probs * (nt(values, upstream) - delta) * scale).astype(jnp.bfloat16)
        d_khat = jnp.dot(d_scores, queries, preferred_element_type=jnp.float32)
        raw = k_raw[:, at(h)]
        put(late, norm_back(raw, inv_rms(raw), k_gain, d_khat))

    share = gx_ref.shape[0]

    def h_copy(step):
        peer = head_peer(step)
        return remote(
            gx_acc.at[pl.ds(pl.multiple_of(peer * share, share), share)],
            gx_recv.at[step - 1], h_ss.at[step - 1], h_rs.at[step - 1], {"head": peer},
        )

    gx_out = pltpu.make_async_copy(gx_buf, gx_ref, gx_sem.at[0])

    def gw_copy(c):
        kind, where = place(c)
        return pltpu.make_async_copy(gw_buf.at[c], gw_ref.at[kind, :, where], gw_sem.at[c])

    def finish(c):
        gw_buf[c] = part[c, me_seq]
        for side in range(2):
            @pl.when(fed[side])
            def _():
                hop(side, c, me_seq).wait_recv()
                gw_buf[c] += flow[side, c, me_seq].astype(jnp.float32)
        gw_copy(c).start()

    @pl.loop(0, chunks + n_seq)
    def _(tick):
        @pl.when(tick < chunks)
        def _():
            with scope("WSHARE"):
                weight_share(tick)

        for side in range(2):
            lag = n_seq - 1 - me_seq if side else me_seq
            c = tick - lag

            @pl.when((c >= 0) & (c < chunks))
            def _():
                with scope("STAGE%d" % side):
                    stage(side, c)

        @pl.when(tick == 0)
        def _():
            with scope("HALOQ"):
                @pl.loop(0, parts)
                def _(p):
                    halo_part(0, pieces - 1, p)

            @pl.when(above)
            def _():
                with scope("DOW"):
                    do_copy(0).wait_recv()
                    stat_copy(0).wait_recv()

            @pl.when(below)
            def _():
                with scope("DOW"):
                    do_copy(1).wait_recv()
                    stat_copy(1).wait_recv()

        @pl.when(tick < parts)
        def _():
            with scope("REV"):
                @pl.loop(0, group)
                def _(j):
                    reverse(tick * group + j)

        for j in range(group):
            @pl.when(tick < chunks - early // group)
            def _():
                with scope("PASSON"):
                    pass_on(tick * group + j + early)

            @pl.when(tick < chunks - parts)
            def _():
                send_own(tick * group + j + heads)

        @pl.when(tick < chunks)
        def _():
            with scope("INSHARE"):
                input_share(tick)

        @pl.when(tick == chunks - 1)
        def _():
            for step in range(1, n_head):
                h_copy(step).start()

        @pl.when(tick == chunks)
        def _():
            with scope("GX"):
                for step in range(1, n_head):
                    h_copy(step).wait()
                total = gx_acc[pl.ds(pl.multiple_of(me_head * share, share), share)]
                for step in range(1, n_head):
                    total = total + gx_recv[step - 1]
                gx_buf[...] = total.astype(gx_buf.dtype)
                gx_out.start()

        @pl.when(tick >= n_seq)
        def _():
            with scope("FINAL"):
                finish(tick - n_seq)

    with scope("SETTLE"):
        @pl.loop(0, chunks)
        def _(c):
            gw_copy(c).wait()
            for side in range(2):
                @pl.loop(0, n_seq)
                def _(t):
                    @pl.when(onward(side, t))
                    def _():
                        hop(side, c, t).wait_send()

        @pl.loop(0, items)
        def _(i):
            for step in direct:
                dp_copy(i, step).wait_send()
                if relay:
                    relay_copy(i, step).wait_send()

        @pl.loop(0, parts)
        def _(p):
            out_copy(p).wait()

        gx_out.wait()

        def settle(side):
            do_copy(side).wait_send()
            stat_copy(side).wait_send()
            for j in range(pieces):
                lat_copy(side, j).wait_send()
                for step in range(1, n_head):
                    pass_copy(side, j, step).wait_send()

        @pl.when(below)
        def _():
            settle(0)

        @pl.when(above)
        def _():
            settle(1)

        for step in range(1, n_dp):
            clip_copy(step).wait_send()


def layer(slab_tokens, w_three, q_gain, k_gain, neighbours, upstream):
    n_dp, n_seq, n_head = (lax.axis_size(axis) for axis in ("dp", "seq", "head"))
    slab = slab_tokens.shape[0]
    three, model_width, head_width = w_three.shape
    heads = head_width // HD
    group = 2 if heads % 2 == 0 else 1
    width = group * HD
    chunks = three * heads // group
    items = three * heads
    block = model_width // n_dp
    rows = block // n_seq
    share = slab // n_head
    pieces = PIECES
    piece = slab // pieces
    stat_rows = -(-2 * heads // 8) * 8
    relays = 4 if n_dp == 4 else n_dp - 1
    anywhere = pl.BlockSpec(memory_space=pl.ANY)
    in_hbm = pl.BlockSpec(memory_space=pltpu.MemorySpace.HBM)
    dma = pltpu.SemaphoreType.DMA
    bf16, f32 = jnp.bfloat16, jnp.float32
    return pl.pallas_call(
        functools.partial(layer_kernel, n_dp, n_seq, n_head),
        out_shape=(
            jax.ShapeDtypeStruct((slab, head_width), bf16),
            jax.ShapeDtypeStruct((three, rows, head_width), f32),
            jax.ShapeDtypeStruct((share, model_width), bf16),
        ),
        in_specs=[in_hbm] * 6,
        out_specs=(anywhere,) * 3,
        scratch_shapes=[
            pltpu.VMEM((items, n_dp, slab, HD), bf16),
            pltpu.VMEM((block, n_dp * slab), bf16),
            pltpu.VMEM((chunks, n_seq, rows, width), f32),
            pltpu.VMEM((2, chunks, n_seq, rows, width), bf16),
            pltpu.VMEM((slab, model_width), f32),
            pltpu.VMEM((n_head - 1, share, model_width), f32),
            pltpu.VMEM((share, model_width), bf16),
            pltpu.VMEM((slab, model_width), bf16),
            pltpu.VMEM((pieces, 2, piece, model_width), bf16),
            pltpu.VMEM((three, model_width, head_width), bf16),
            pltpu.VMEM((3, slab, head_width), bf16),
            pltpu.VMEM((slab, head_width), f32),
            pltpu.VMEM((slab, head_width), f32),
            pltpu.VMEM((3, slab, head_width), bf16),
            pltpu.VMEM((3, slab, head_width), bf16),
            pltpu.VMEM((3, slab, head_width), bf16),
            pltpu.VMEM((slab, 3 * slab), f32),
            pltpu.VMEM((slab, 3 * slab), f32),
            pltpu.VMEM((slab, 128), f32),
            pltpu.VMEM((3, stat_rows, slab), f32),
            pltpu.VMEM((n_dp - 1, slab, block), bf16),
            pltpu.VMEM((slab, head_width), bf16),
            pltpu.VMEM((chunks, rows, width), f32),
            pltpu.VMEM((1, HD), f32),
            pltpu.VMEM((1, HD), f32),
            pltpu.VMEM(neighbours.shape, jnp.int32),
            dma((5,)),
            dma((chunks,)),
            dma((2, pieces)),
            dma((2, pieces)),
            dma((2, pieces, n_head - 1)),
            dma((2, pieces, n_head - 1)),
            dma((2,)),
            dma((2,)),
            dma((2,)),
            dma((2,)),
            dma((n_dp - 1,)),
            dma((n_dp - 1,)),
            dma((items, relays)),
            dma((items, relays)),
            dma((2, chunks, n_seq)),
            dma((2, chunks, n_seq)),
            dma((n_head - 1,)),
            dma((n_head - 1,)),
            dma((chunks // three,)),
            dma((chunks,)),
            dma((1,)),
        ],
        compiler_params=pltpu.CompilerParams(
            collective_id=0, has_side_effects=True, vmem_limit_bytes=52 * 1024 * 1024
        ),
        name="layer",
    )(slab_tokens, w_three, q_gain.reshape(1, HD), k_gain.reshape(1, HD), neighbours, upstream)


def local(latents, w_qkv, q_gain, k_gain, neighbours, grad_out):
    w_three = jnp.transpose(w_qkv, (1, 0, 2))
    attn_out, grad_w, grad_x = layer(
        latents[0], w_three, q_gain, k_gain, neighbours, grad_out[0]
    )
    return (attn_out[None], grad_x[None], jnp.transpose(grad_w, (1, 0, 2)))


def solution(mesh):
    in_specs = (P("dp", "seq", None), P(None, None, "head"), P(), P(), P(), P("dp", "seq", "head"))
    out_specs = (
        P("dp", "seq", "head"),
        P("dp", ("seq", "head"), None),
        P(("dp", "seq"), None, "head"),
    )
    return jax.shard_map(local, mesh=mesh, in_specs=in_specs, out_specs=out_specs, check_vma=False)
```

time: 100 us -> 101 us (1.010)
    unnamed x5 -> x13, local copies, waits for them, and re-layouts: 4.76 us -> 5.55 us
where the time goes in v1:
time: 101 us; the launch traced here: 100 us
  Pallas kernels  94.2 us (93%)
  local copies, waits for them, and re-layouts  5.55 us (5%)
    pallas_call x1, Pallas kernels, layer(): pl.pallas_call(functools.partial(layer_kernel, n_dp, n_seq, n_head), out_...  94.2 us
    unnamed x13, local copies, waits for them, and re-layouts  5.55 us

profile of v1, /device:TPU:0, one launch (start us, length us, event | category | flops | bytes accessed | tf_op | source)
XLA Modules:
  0.0 100.5 jit_solution(14321202878234429145)
XLA Ops:
  0.6 0.0 copy-start
  0.6 1.0 copy-done
  1.6 0.0 copy-start.1
  1.6 0.7 copy-done.1
  2.3 0.0 copy-start.2
  2.3 0.7 copy-done.2
  3.0 0.0 copy-start.3
  3.0 0.7 copy-done.3
  3.6 94.2 %layer.1 = (bf16[256,768]{1,0:T(8,128)(2,1)S(1)}, f32[3,128,768]{2,1,0:T(8,128)}, bf16[128,2048]{1,0:T(8,128)(2,1)S(1)}) custom-call(bf16[256,2048]{1,0:T(8,128)(2,1)} %bitcast.15, bf16[3,2048,768]{2,1,0:T(8,128)(2,1)} %bitcast.13, f32[1,128]{1,0:T(1,128)S(1)} %bitcast.11, f32[1,128]{1,0:T(1,128)S(1)} %bitcast.12, s32[16,9]{1,0:T(8,128)S(1)} %copy-done.1, ...), custom_call_target="tpu_custom_call" | custom-call | tf_op jit(solution)/shard_map/layer/pallas_call | solution.py:650
  97.9 0.0 copy-start.4
  97.9 0.7 copy.12
  98.7 0.8 copy.13
  99.4 0.0 copy-done.4
  99.4 1.0 %copy.14 = f32[128,3,768]{2,0,1:T(8,128)} copy(f32[128,3,768]{2,0,1:T(8,128)S(1)} %bitcast.14) | data formatting | bytes 2359296
Async XLA Ops:
  0.6 1.0 copy-start
  1.6 0.7 copy-start.1
  2.3 0.7 copy-start.2
  3.0 0.7 copy-start.3
  97.9 1.6 %copy-start.4 = (f32[3,128,768]{2,1,0:T(8,128)S(1)}, f32[3,128,768]{2,1,0:T(8,128)}, u32[]{:S(2)}) copy-start(f32[3,128,768]{2,1,0:T(8,128)} %get-tuple-element.8) | copy-start | bytes 3538948

commit v2 on v1

--- a/solution.py
+++ b/solution.py
@@ -14,7 +14,11 @@
 HD = 128
 TILE = 64
 PIECES = 2
-AHEAD = 2
+PASS_LAG = 2
+PRODUCT_LAG = 4
+HOP_LAG = 2
+NEAR_LAST = 8
+STATS = 4
 
 
 EPS = 1e-06
@@ -47,6 +51,10 @@
         device_id=peer,
         device_id_type=MESH,
     )
+
+
+def drain(ref, sem):
+    pltpu.make_async_copy(ref, ref, sem).wait()
 
 
 def layer_kernel(
@@ -60,11 +68,12 @@
 ):
     three, model_width, head_width = w_ref.shape
     slab = lat_ref.shape[0]
-    items = gath.shape[0]
-    chunks, _, rows, width = part.shape
-    group = width // HD
-    parts = chunks // three
+    items, _, rows, _ = part.shape
     heads = head_width // HD
+    group = 2 if heads % 2 == 0 else 1
+    width = group * HD
+    parts = heads // group
+    chunks = three * parts
     pieces, _, piece, _ = halo.shape
     sub = piece // n_head
     block = model_width // n_dp
@@ -121,18 +130,14 @@
         pltpu.make_async_copy(kg_ref, kg_buf, l_sem.at[4]),
     ]
 
-    def w_copy(kind, p):
-        return pltpu.make_async_copy(
-            w_ref.at[kind, :, cols(p)], w_buf.at[kind, :, cols(p)], w_sem.at[kind * parts + p]
-        )
+    def w_copy(kind):
+        return pltpu.make_async_copy(w_ref.at[kind], w_buf.at[kind], w_sem.at[kind])
 
     for copy in small:
         copy.start()
     own_lat.start()
     for kind in range(three):
-        @pl.loop(0, parts)
-        def _(p):
-            w_copy(kind, p).start()
+        w_copy(kind).start()
     own_do.start()
 
     for copy in small:
@@ -188,7 +193,7 @@
         return remote(
             lat_ref.at[pl.ds(pl.multiple_of(j * piece + me_head * sub, sub), sub)],
             halo.at[j, 1 - side, sub_rows],
-            a_ss.at[side, j], a_rs.at[side, j], {"seq": me_seq + 2 * side - 1},
+            a_ss.at[side], a_rs.at[side, j], {"seq": me_seq + 2 * side - 1},
         )
 
     def do_copy(side):
@@ -197,16 +202,19 @@
             o_ss.at[side], o_rs.at[side], {"seq": me_seq + 2 * side - 1},
         )
 
-    def stat_copy(side):
+    def stat_rows(m):
+        return pl.ds(pl.multiple_of(m * 2 * STATS, 2 * STATS), 2 * STATS)
+
+    def stat_copy(side, m):
         return remote(
-            stat_t.at[1], stat_t.at[2 - 2 * side],
-            s_ss.at[side], s_rs.at[side], {"seq": me_seq + 2 * side - 1},
+            stat_t.at[1, stat_rows(m)], stat_t.at[2 - 2 * side, stat_rows(m)],
+            s_ss.at[side], s_rs.at[side, m], {"seq": me_seq + 2 * side - 1},
         )
 
     def pass_copy(side, j, step):
         return remote(
             halo.at[j, side, sub_rows], halo.at[j, side, sub_rows],
-            f_ss.at[side, j, step - 1], f_rs.at[side, j, step - 1],
+            f_ss.at[side, step - 1], f_rs.at[side, j, step - 1],
             {"head": head_peer(step)},
         )
 
@@ -214,7 +222,7 @@
         peer = dp_peer(step)
         return remote(
             lat_ref.at[:, pl.ds(pl.multiple_of(peer * block, block), block)],
-            clip_buf.at[step - 1], c_ss.at[step - 1], c_rs.at[step - 1], {"dp": peer},
+            clip_buf.at[step - 1], c_ss.at[0], c_rs.at[step - 1], {"dp": peer},
         )
 
     for j in range(pieces):
@@ -248,9 +256,10 @@
 
     for kind in range(three):
         with scope("OWN%d" % kind):
+            w_copy(kind).wait()
+
             @pl.loop(0, parts)
             def _(p):
-                w_copy(kind, p).wait()
                 raw = jnp.dot(
                     lat_own[...], w_buf[kind, :, cols(p)], preferred_element_type=jnp.float32
                 )
@@ -308,18 +317,26 @@
                 def _(p):
                     halo_part(kind, j, p)
 
+    own_cols = pl.ds(pl.multiple_of(me_dp * block, block), block)
+    with scope("CLIP"):
+        latt_ref[:, :slab] = jnp.transpose(lat_own[:, own_cols])
+        for step in range(1, n_dp):
+            clip_copy(step).wait_recv()
+            latt_ref[:, step * slab : (step + 1) * slab] = jnp.transpose(clip_buf[step - 1])
+
+    gx_acc[...] = jnp.zeros_like(gx_acc)
+
     with scope("ARRIVEL"):
         arrive(pieces - 1)
 
     def put(item, value):
         gath[item, 0] = value.astype(jnp.bfloat16)
 
-    def place(position):
-        late = jnp.maximum(position - parts, 0)
-        is_late = jnp.where(position >= parts, 1, 0)
+    def place(i):
+        late = jnp.maximum(i - heads, 0)
+        is_late = jnp.where(i >= heads, 1, 0)
         kind = is_late * (1 + lax.rem(late, 2))
-        p = is_late * (late // 2) + (1 - is_late) * position
-        return kind, cols(p)
+        return kind, is_late * (late // 2) + (1 - is_late) * i
 
     relay = n_dp == 4
     direct = (1, 2) if relay else tuple(range(1, n_dp))
@@ -329,14 +346,14 @@
     def dp_copy(i, step):
         return remote(
             gath.at[i, 0], gath.at[i, step],
-            d_ss.at[i, step - 1], d_rs.at[i, step - 1], {"dp": dp_peer(step)},
+            d_ss.at[step - 1], d_rs.at[i, step - 1], {"dp": dp_peer(step)},
         )
 
     def relay_copy(i, via):
         which = (first, second)[via - 1]
         return remote(
             gath.at[i, via, which], gath.at[i, 3, which],
-            d_ss.at[i, 1 + via], d_rs.at[i, 1 + via], {"dp": dp_peer(3 - via)},
+            d_ss.at[1 + via], d_rs.at[i, 1 + via], {"dp": dp_peer(3 - via)},
         )
 
     def send_own(i):
@@ -353,49 +370,66 @@
         peer = lax.rem(me_seq + n_seq + 1 - 2 * side, n_seq)
         return remote(
             flow.at[side, c, t], flow.at[side, c, t],
-            z_ss.at[side, c, t], z_rs.at[side, c, t], {"seq": peer},
+            z_ss.at[side, t], z_rs.at[side, c, t], {"seq": peer},
         )
 
     fed = (below, above)
 
     def onward(side, t):
         return t < me_seq if side else t > me_seq
+
+    def hand_on(side, c, t):
+        @pl.when(onward(side, t))
+        def _():
+            @pl.when(fed[side])
+            def _():
+                hop(side, c, t).wait_recv()
+                summed = part[c, t] + flow[side, c, t].astype(jnp.float32)
+                flow[side, c, t] = summed.astype(jnp.bfloat16)
+
+            @pl.when(jnp.logical_not(fed[side]))
+            def _():
+                flow[side, c, t] = part[c, t].astype(jnp.bfloat16)
+
+            hop(side, c, t).start()
+
+    def near(side):
+        return me_seq - 1 if side else me_seq + 1
 
     def stage(side, c):
         @pl.loop(0, n_seq)
         def _(turn):
             t = turn if side else n_seq - 1 - turn
 
-            @pl.when(onward(side, t))
+            @pl.when((t != near(side)) | fed[side] | (c < items - NEAR_LAST))
             def _():
-                @pl.when(fed[side])
-                def _():
-                    hop(side, c, t).wait_recv()
-                    summed = part[c, t] + flow[side, c, t].astype(jnp.float32)
-                    flow[side, c, t] = summed.astype(jnp.bfloat16)
-
-                @pl.when(jnp.logical_not(fed[side]))
-                def _():
-                    flow[side, c, t] = part[c, t].astype(jnp.bfloat16)
-
-                hop(side, c, t).start()
-
-    def paired(ref, c):
-        found = [ref(c * group + j) for j in range(group)]
-        return jnp.concatenate(found, axis=1)
+                hand_on(side, c, t)
+
+        @pl.when((c == items - 1) & jnp.logical_not(fed[side]))
+        def _():
+            @pl.loop(max(items - NEAR_LAST, 0), items)
+            def _(late):
+                hand_on(side, late, near(side))
 
     def input_share(c):
-        kind, where = place(c)
-        gx_acc[...] += nt(paired(lambda i: gath[i, 0], c), w_buf[kind, :, where])
-
-    def weight_share(c):
+        late = jnp.maximum(c - parts, 0)
+        is_late = jnp.where(c >= parts, 1, 0)
+        kind = is_late * (1 + lax.rem(late, 2))
+        p = is_late * (late // 2) + (1 - is_late) * c
+        found = []
+        for j in range(group):
+            h = p * group + j
+            found.append(gath[is_late * (heads + h + kind - 1) + h, 0])
+        gx_acc[...] += nt(jnp.concatenate(found, axis=1), w_buf[kind, :, cols(p)])
+
+    def weight_share(i):
         if relay:
-            for j in range(group):
-                for via in (1, 2):
-                    relay_copy(c * group + j, via).wait_recv()
-        everyone = paired(lambda i: gath[i].reshape(n_dp * slab, HD), c)
-        product = jnp.dot(latt_ref[...], everyone, preferred_element_type=jnp.float32)
-        part[c] = product.reshape(n_seq, rows, width)
+            for via in (1, 2):
+                relay_copy(i, via).wait_recv()
+        product = jnp.dot(
+            latt_ref[...], gath[i].reshape(n_dp * slab, HD), preferred_element_type=jnp.float32
+        )
+        part[i] = product.reshape(n_seq, rows, HD)
 
     own_do.wait()
     lanes = lax.broadcasted_iota(jnp.int32, (slab, 128), 1)
@@ -403,7 +437,7 @@
 
     def out_copy(p):
         return pltpu.make_async_copy(
-            out_buf.at[:, cols(p)], out_ref.at[:, cols(p)], out_sem.at[p]
+            out_buf.at[:, cols(p)], out_ref.at[:, cols(p)], out_sem.at[0]
         )
 
     def forward(h):
@@ -425,45 +459,6 @@
         kept = jnp.where(lanes == 2 * h, row_total, stat[...])
         stat[...] = jnp.where(lanes == 2 * h + 1, row_delta, kept)
 
-    early = max(heads - AHEAD * group, 0)
-
-    @pl.loop(0, parts)
-    def _(p):
-        with scope("HALOKV"):
-            halo_part(1, pieces - 1, p)
-            halo_part(2, pieces - 1, p)
-
-        @pl.loop(0, group)
-        def _(j):
-            h = p * group + j
-            with scope("FWD"):
-                forward(h)
-                send_own(h)
-
-            @pl.when(h >= heads - early)
-            def _():
-                with scope("PASSE"):
-                    pass_on(h - (heads - early))
-
-        out_copy(p).start()
-
-    stat_t[1] = jnp.transpose(stat[...])[: stat_t.shape[1]]
-
-    @pl.when(below)
-    def _():
-        stat_copy(0).start()
-
-    @pl.when(above)
-    def _():
-        stat_copy(1).start()
-
-    own_cols = pl.ds(pl.multiple_of(me_dp * block, block), block)
-    with scope("CLIP"):
-        latt_ref[:, :slab] = jnp.transpose(lat_own[:, own_cols])
-        for step in range(1, n_dp):
-            clip_copy(step).wait_recv()
-            latt_ref[:, step * slab : (step + 1) * slab] = jnp.transpose(clip_buf[step - 1])
-
     gx_acc[...] = jnp.zeros_like(gx_acc)
 
     def reverse(h):
@@ -474,8 +469,8 @@
         total = jnp.concatenate([stat_t[s, pl.ds(2 * h, 1), :] for s in range(3)], axis=1)
         delta = jnp.concatenate([stat_t[s, pl.ds(2 * h + 1, 1), :] for s in range(3)], axis=1)
         probs = jnp.exp(nt(keys, queries) * scale) * mask_t[...] * (1.0 / total)
-        late = (parts + 2 * (h // group)) * group + lax.rem(h, group)
-        put(late + group, jnp.dot(probs.astype(jnp.bfloat16), upstream, preferred_element_type=jnp.float32))
+        late = heads + 2 * h
+        put(late + 1, jnp.dot(probs.astype(jnp.bfloat16), upstream, preferred_element_type=jnp.float32))
         d_scores = (probs * (nt(values, upstream) - delta) * scale).astype(jnp.bfloat16)
         d_khat = jnp.dot(d_scores, queries, preferred_element_type=jnp.float32)
         raw = k_raw[:, at(h)]
@@ -492,9 +487,9 @@
 
     gx_out = pltpu.make_async_copy(gx_buf, gx_ref, gx_sem.at[0])
 
-    def gw_copy(c):
-        kind, where = place(c)
-        return pltpu.make_async_copy(gw_buf.at[c], gw_ref.at[kind, :, where], gw_sem.at[c])
+    def gw_copy(i):
+        kind, h = place(i)
+        return pltpu.make_async_copy(gw_buf.at[i], gw_ref.at[kind, :, at(h)], gw_sem.at[0])
 
     def finish(c):
         gw_buf[c] = part[c, me_seq]
@@ -505,126 +500,202 @@
                 gw_buf[c] += flow[side, c, me_seq].astype(jnp.float32)
         gw_copy(c).start()
 
-    @pl.loop(0, chunks + n_seq)
-    def _(tick):
-        @pl.when(tick < chunks)
-        def _():
-            with scope("WSHARE"):
-                weight_share(tick)
-
+    def settle_items():
+        for step in direct:
+            drain(gath.at[:, 0], d_ss.at[step - 1])
+            if relay:
+                drain(gath.at[:, 0, first], d_ss.at[1 + step])
+        drain(out_buf, out_sem.at[0])
+        drain(clip_buf, c_ss.at[0])
+
+        def settle(side):
+            do_copy(side).wait_send()
+            drain(stat_t.at[1], s_ss.at[side])
+            drain(halo.at[:, side, pl.ds(0, sub)], a_ss.at[side])
+            for step in range(1, n_head):
+                drain(halo.at[:, side, pl.ds(0, sub)], f_ss.at[side, step - 1])
+
+        @pl.when(below)
+        def _():
+            settle(0)
+
+        @pl.when(above)
+        def _():
+            settle(1)
+
+    def settle_hops():
+        for side in range(2):
+            @pl.loop(0, n_seq)
+            def _(t):
+                @pl.when(onward(side, t))
+                def _():
+                    drain(flow.at[side, :, t], z_ss.at[side, t])
+
+    product_end = items + PRODUCT_LAG
+    gx_tick = heads + 2 * heads - 1 + 2 * parts
+    ticks = max(product_end + HOP_LAG * max(n_seq - 2, 0), gx_tick + 1)
+    finish_lag = product_end + HOP_LAG * (n_seq - 1) + 1 - items
+    in_loop = max(min(items - NEAR_LAST, ticks - finish_lag), 0)
+
+    def product(tick):
+        with scope("WSHARE"):
+            weight_share(tick - PRODUCT_LAG)
+
+    def stages(tick):
         for side in range(2):
             lag = n_seq - 1 - me_seq if side else me_seq
-            c = tick - lag
-
-            @pl.when((c >= 0) & (c < chunks))
+            c = tick - PRODUCT_LAG - HOP_LAG * lag
+
+            @pl.when((c >= 0) & (c < items))
             def _():
                 with scope("STAGE%d" % side):
                     stage(side, c)
 
-        @pl.when(tick == 0)
-        def _():
-            with scope("HALOQ"):
-                @pl.loop(0, parts)
-                def _(p):
-                    halo_part(0, pieces - 1, p)
+    def pass_next(tick):
+        with scope("PASSON"):
+            pass_on(tick - PASS_LAG)
+
+    def query_part(p):
+        with scope("HALOQ"):
+            halo_part(0, pieces - 1, p)
+
+    @pl.loop(0, heads)
+    def _(tick):
+        @pl.when(lax.rem(tick, group) == 0)
+        def _():
+            with scope("HALOKV"):
+                halo_part(1, pieces - 1, tick // group)
+                halo_part(2, pieces - 1, tick // group)
+
+        with scope("FWD"):
+            forward(tick)
+
+        @pl.when((lax.rem(tick, STATS) == STATS - 1) | (tick == heads - 1))
+        def _():
+            m = tick // STATS
+            turned = jnp.transpose(stat[...])
+            for k in range(stat_t.shape[1] // (2 * STATS)):
+                @pl.when(m == k)
+                def _():
+                    at_rows = slice(k * 2 * STATS, (k + 1) * 2 * STATS)
+                    stat_t[1, at_rows] = turned[at_rows]
+
+            @pl.when(below)
+            def _():
+                stat_copy(0, m).start()
 
             @pl.when(above)
             def _():
-                with scope("DOW"):
-                    do_copy(0).wait_recv()
-                    stat_copy(0).wait_recv()
-
-            @pl.when(below)
+                stat_copy(1, m).start()
+
+        @pl.when(tick == heads - 1)
+        def _():
+            query_part(0)
+
+        @pl.when(tick >= PRODUCT_LAG)
+        def _():
+            product(tick)
+            stages(tick)
+
+        @pl.when(tick >= PASS_LAG)
+        def _():
+            pass_next(tick)
+
+        send_own(tick)
+
+        @pl.when(lax.rem(tick, group) == group - 1)
+        def _():
+            out_copy(tick // group).start()
+
+    @pl.loop(heads, ticks)
+    def _(tick):
+        turn = tick - heads
+        odd = lax.rem(turn, 2) == 1
+        reversing = (turn == 0) | odd & (turn < 2 * heads - 1)
+
+        @pl.when(tick < items + PASS_LAG)
+        def _():
+            pass_next(tick)
+
+        for side, has in ((0, above), (1, below)):
+            @pl.when((turn == 0) & has)
             def _():
                 with scope("DOW"):
-                    do_copy(1).wait_recv()
-                    stat_copy(1).wait_recv()
-
-        @pl.when(tick < parts)
+                    do_copy(side).wait_recv()
+
+            @pl.when(reversing & has & (lax.rem((turn + 1) // 2, STATS) == 0))
+            def _():
+                with scope("STW"):
+                    stat_copy(side, (turn + 1) // 2 // STATS).wait_recv()
+
+        @pl.when(reversing)
         def _():
             with scope("REV"):
-                @pl.loop(0, group)
-                def _(j):
-                    reverse(tick * group + j)
-
-        for j in range(group):
-            @pl.when(tick < chunks - early // group)
-            def _():
-                with scope("PASSON"):
-                    pass_on(tick * group + j + early)
-
-            @pl.when(tick < chunks - parts)
-            def _():
-                send_own(tick * group + j + heads)
-
-        @pl.when(tick < chunks)
+                reverse((turn + 1) // 2)
+
+        @pl.when(turn == 0)
+        def _():
+            send_own(heads)
+
+        @pl.when(tick + 1 < items)
+        def _():
+            send_own(tick + 1)
+
+        @pl.when((lax.rem(turn, 2 * group) == 2 * group - 2) & (turn < 2 * heads - 2 * group))
+        def _():
+            query_part((turn + 2) // (2 * group))
+
+        @pl.when((turn >= 2) & jnp.logical_not(odd) & (turn // 2 - 1 < chunks - parts))
         def _():
             with scope("INSHARE"):
-                input_share(tick)
-
-        @pl.when(tick == chunks - 1)
+                input_share(turn // 2 - 1)
+
+        @pl.when(odd & (turn >= 2 * heads - 1) & (turn < 2 * heads - 1 + 2 * parts))
+        def _():
+            with scope("INSHARE"):
+                input_share(chunks - 1 - (turn - 2 * heads + 1) // 2)
+
+        @pl.when(tick < product_end)
+        def _():
+            product(tick)
+
+        stages(tick)
+
+        @pl.when(tick == gx_tick)
         def _():
             for step in range(1, n_head):
                 h_copy(step).start()
 
-        @pl.when(tick == chunks)
-        def _():
-            with scope("GX"):
-                for step in range(1, n_head):
-                    h_copy(step).wait()
-                total = gx_acc[pl.ds(pl.multiple_of(me_head * share, share), share)]
-                for step in range(1, n_head):
-                    total = total + gx_recv[step - 1]
-                gx_buf[...] = total.astype(gx_buf.dtype)
-                gx_out.start()
-
-        @pl.when(tick >= n_seq)
+        c = tick - finish_lag
+
+        @pl.when((c >= 0) & (c < in_loop))
         def _():
             with scope("FINAL"):
-                finish(tick - n_seq)
+                finish(c)
+
+        @pl.when(tick == product_end)
+        def _():
+            with scope("SETTLEI"):
+                settle_items()
+
+    with scope("GX"):
+        for step in range(1, n_head):
+            h_copy(step).wait()
+        total = gx_acc[pl.ds(pl.multiple_of(me_head * share, share), share)]
+        for step in range(1, n_head):
+            total = total + gx_recv[step - 1]
+        gx_buf[...] = total.astype(gx_buf.dtype)
+        gx_out.start()
+
+    @pl.loop(in_loop, items)
+    def _(c):
+        with scope("FINAL"):
+            finish(c)
 
     with scope("SETTLE"):
-        @pl.loop(0, chunks)
-        def _(c):
-            gw_copy(c).wait()
-            for side in range(2):
-                @pl.loop(0, n_seq)
-                def _(t):
-                    @pl.when(onward(side, t))
-                    def _():
-                        hop(side, c, t).wait_send()
-
-        @pl.loop(0, items)
-        def _(i):
-            for step in direct:
-                dp_copy(i, step).wait_send()
-                if relay:
-                    relay_copy(i, step).wait_send()
-
-        @pl.loop(0, parts)
-        def _(p):
-            out_copy(p).wait()
-
+        settle_hops()
+        drain(gw_buf, gw_sem.at[0])
         gx_out.wait()
-
-        def settle(side):
-            do_copy(side).wait_send()
-            stat_copy(side).wait_send()
-            for j in range(pieces):
-                lat_copy(side, j).wait_send()
-                for step in range(1, n_head):
-                    pass_copy(side, j, step).wait_send()
-
-        @pl.when(below)
-        def _():
-            settle(0)
-
-        @pl.when(above)
-        def _():
-            settle(1)
-
-        for step in range(1, n_dp):
-            clip_copy(step).wait_send()
 
 
 def layer(slab_tokens, w_three, q_gain, k_gain, neighbours, upstream):
@@ -632,9 +703,6 @@
     slab = slab_tokens.shape[0]
     three, model_width, head_width = w_three.shape
     heads = head_width // HD
-    group = 2 if heads % 2 == 0 else 1
-    width = group * HD
-    chunks = three * heads // group
     items = three * heads
     block = model_width // n_dp
     rows = block // n_seq
@@ -659,8 +727,8 @@
         scratch_shapes=[
             pltpu.VMEM((items, n_dp, slab, HD), bf16),
             pltpu.VMEM((block, n_dp * slab), bf16),
-            pltpu.VMEM((chunks, n_seq, rows, width), f32),
-            pltpu.VMEM((2, chunks, n_seq, rows, width), bf16),
+            pltpu.VMEM((items, n_seq, rows, HD), f32),
+            pltpu.VMEM((2, items, n_seq, rows, HD), bf16),
             pltpu.VMEM((slab, model_width), f32),
             pltpu.VMEM((n_head - 1, share, model_width), f32),
             pltpu.VMEM((share, model_width), bf16),
@@ -679,44 +747,72 @@
             pltpu.VMEM((3, stat_rows, slab), f32),
             pltpu.VMEM((n_dp - 1, slab, block), bf16),
             pltpu.VMEM((slab, head_width), bf16),
-            pltpu.VMEM((chunks, rows, width), f32),
+            pltpu.VMEM((items, rows, HD), f32),
             pltpu.VMEM((1, HD), f32),
             pltpu.VMEM((1, HD), f32),
             pltpu.VMEM(neighbours.shape, jnp.int32),
             dma((5,)),
-            dma((chunks,)),
+            dma((three,)),
+            dma((2,)),
             dma((2, pieces)),
-            dma((2, pieces)),
-            dma((2, pieces, n_head - 1)),
+            dma((2, n_head - 1)),
             dma((2, pieces, n_head - 1)),
             dma((2,)),
             dma((2,)),
             dma((2,)),
-            dma((2,)),
+            dma((2, stat_rows // (2 * STATS))),
+            dma((1,)),
             dma((n_dp - 1,)),
-            dma((n_dp - 1,)),
+            dma((relays,)),
             dma((items, relays)),
-            dma((items, relays)),
-            dma((2, chunks, n_seq)),
-            dma((2, chunks, n_seq)),
+            dma((2, n_seq)),
+            dma((2, items, n_seq)),
             dma((n_head - 1,)),
             dma((n_head - 1,)),
-            dma((chunks // three,)),
-            dma((chunks,)),
+            dma((1,)),
+            dma((1,)),
             dma((1,)),
         ],
         compiler_params=pltpu.CompilerParams(
-            collective_id=0, has_side_effects=True, vmem_limit_bytes=52 * 1024 * 1024
+            collective_id=0, has_side_effects=True, vmem_limit_bytes=48 * 1024 * 1024
         ),
         name="layer",
-    )(slab_tokens, w_three, q_gain.reshape(1, HD), k_gain.reshape(1, HD), neighbours, upstream)
+    )(slab_tokens, w_three, q_gain, k_gain, neighbours, upstream)
+
+
+def deliver_kernel(*refs):
+    count = len(refs) // 3
+    sources, targets, sems = refs[:count], refs[count : 2 * count], refs[2 * count :]
+    copies = [pltpu.make_async_copy(*three) for three in zip(sources, targets, sems)]
+    for copy in copies:
+        copy.start()
+    for copy in copies:
+        copy.wait()
+
+
+def deliver(*arrays):
+    anywhere = pl.BlockSpec(memory_space=pl.ANY)
+    return pl.pallas_call(
+        deliver_kernel,
+        out_shape=tuple(jax.ShapeDtypeStruct(x.shape, x.dtype) for x in arrays),
+        in_specs=[anywhere] * len(arrays),
+        out_specs=(anywhere,) * len(arrays),
+        scratch_shapes=[pltpu.SemaphoreType.DMA] * len(arrays),
+        compiler_params=pltpu.CompilerParams(vmem_limit_bytes=1024 * 1024),
+        name="deliver",
+    )(*arrays)
 
 
 def local(latents, w_qkv, q_gain, k_gain, neighbours, grad_out):
     w_three = jnp.transpose(w_qkv, (1, 0, 2))
-    attn_out, grad_w, grad_x = layer(
-        latents[0], w_three, q_gain, k_gain, neighbours, grad_out[0]
+    latents, w_three, q_gain, k_gain, neighbours, grad_out = (
+        pltpu.with_memory_space_constraint(x, pltpu.MemorySpace.HBM)
+        for x in (
+            latents[0], w_three, q_gain.reshape(1, HD), k_gain.reshape(1, HD), neighbours, grad_out[0]
+        )
     )
+    found = layer(latents, w_three, q_gain, k_gain, neighbours, grad_out)
+    attn_out, grad_w, grad_x = deliver(*found)
     return (attn_out[None], grad_x[None], jnp.transpose(grad_w, (1, 0, 2)))
 
 

time: 101 us -> 80.4 us (0.80)
  Pallas kernels: 94.2 us -> 79.5 us
  local copies, waits for them, and re-layouts: 5.55 us -> 0 us
    pallas_call x1, Pallas kernels: 94.2 us -> 78.2 us  [layer(): pl.pallas_call(functools.partial(layer_kernel, n_dp, n_seq, n_head), out_...]
    unnamed x13 -> x0, local copies, waits for them, and re-layouts: 5.55 us -> none
    pallas_call x0 -> x1, Pallas kernels: none -> 1.34 us  [deliver(): pl.pallas_call(deliver_kernel, out_shape=tuple((jax.ShapeDtypeStruct(x.sh...]
where the time goes in v2:
time: 80.4 us; the launch traced here: 80.2 us
  Pallas kernels  79.5 us (99%)
    pallas_call x1, Pallas kernels, layer(): pl.pallas_call(functools.partial(layer_kernel, n_dp, n_seq, n_head), out_...  78.2 us

profile of v2, /device:TPU:0, one launch (start us, length us, event | category | flops | bytes accessed | tf_op | source)
XLA Modules:
  0.0 80.2 jit_solution(15425545940809151643)
XLA Ops:
  0.6 78.2 %layer.1 = (bf16[256,768]{1,0:T(8,128)(2,1)S(1)}, f32[3,128,768]{2,1,0:T(8,128)S(1)}, bf16[128,2048]{1,0:T(8,128)(2,1)S(1)}) custom-call(bf16[256,2048]{1,0:T(8,128)(2,1)} %bitcast.9, bf16[3,2048,768]{2,1,0:T(8,128)(2,1)} %bitcast.8, f32[1,128]{1,0:T(1,128)} %bitcast.11, f32[1,128]{1,0:T(1,128)} %bitcast.12, s32[16,9]{1,0:T(8,128)} %near_ref.1, ...), custom_call_target="tpu_custom_call" | custom-call | tf_op jit(solution)/shard_map/layer/pallas_call | solution.py:718
  78.8 1.3 %deliver.1 = (bf16[256,768]{1,0:T(8,128)(2,1)}, f32[3,128,768]{2,1,0:T(8,128)}, bf16[128,2048]{1,0:T(8,128)(2,1)}) custom-call(bf16[256,768]{1,0:T(8,128)(2,1)S(1)} %get-tuple-element.9.refs_0_, f32[3,128,768]{2,1,0:T(8,128)S(1)} %get-tuple-element.10.refs_1_, bf16[128,2048]{1,0:T(8,128)(2,1)S(1)} %get-tuple-element.11.refs_2_), custom_call_target="tpu_custom_call" | custom-call | tf_op jit(solution)/shard_map/deliver/pallas_call | solution.py:795
